TPU v7x, 256 devices: a whole 4x4x8 slice. The times are simulated.
256 devices in a mesh: mic: 64 (over x, z_hi, y), proj: 4 (over z_lo, core).
Axes of the slice: x: 4, y: 4, z: 8 (z_hi: 4, z_lo: 2; z = z_hi * 2 + z_lo), core: 2. Of those that a mesh axis runs over, the one named last changes fastest.
Arguments:
- map_slabs: bfloat16 [20, 8, 256, 256], P('proj'), may hold values from -1.25 to 1.25
- slot_slab: int32 [20], P('proj'), may hold values from -1 to 11, as said below
- orient_index: int32 [4], replicated, may hold values from 0 to 255
- slab_lo: int32 [4], replicated, may hold values from 0 to 4
- slab_hi: int32 [4], replicated, may hold values from 8 to 12
- tile_spectrum: bfloat16 [256, 512, 1024], P(('mic', 'proj')), may hold values from -6 to 6
- prev_max: float32 [256, 512, 512], P(('mic', 'proj')), may hold values from -6 to 6
- prev_sum: float32 [256, 512, 512], P(('mic', 'proj')), may hold values from -12 to 12
- prev_sumsq: float32 [256, 512, 512], P(('mic', 'proj')), may hold values from 0.5 to 4
Outputs:
- best_score: float32 [256, 512, 512], P(('mic', 'proj'))
- score_sum: float32 [256, 512, 512], P(('mic', 'proj'))
- score_sumsq: float32 [256, 512, 512], P(('mic', 'proj'))
Inputs may be any that keep to these rules, and one draw needn't show every extreme that they name: `slot_slab`: each slab 0 to 11 stands in exactly one slot; every other slot holds -1. One index of proj holds 5 slabs; the others may hold fewer, and may hold none.
All inputs are finite; a program needn't handle non-finite values.
Results may differ from a plain program's by a relative error of at most 0.0057.
Values may be sent and summed in bfloat16 or wider, within the bound.
A program may use at most 128 MiB of HBM per device.

v0:
```python
import math

import jax
import jax.numpy as jnp
from jax import lax
from jax.sharding import PartitionSpec as P

SLAB_Z = 8
SLABS = 12
NORI = 256


max_slope = 0.5
golden_angle = 2.399963


def matmul(left_op, right_op):
    return jnp.dot(left_op, right_op, preferred_element_type=jnp.float32)


def tent_weight(offsets):
    return jnp.maximum(0.0, 1.0 - jnp.abs(offsets))


def orient_slopes(orient_index):
    search_step = orient_index.astype(jnp.float32)
    radius = max_slope * jnp.sqrt((search_step + 0.5) / NORI)
    return (
        radius * jnp.cos(golden_angle * search_step),
        radius * jnp.sin(golden_angle * search_step),
    )


def phase_parts(freq_count, pixel_count, length):
    freqs = jnp.arange(freq_count, dtype=jnp.int32)[:, None]
    pixels = jnp.arange(pixel_count, dtype=jnp.int32)[None, :]
    turn_frac = (freqs * pixels % length).astype(jnp.float32) / length
    norm_scale = 1.0 / math.sqrt(length)
    return (
        jnp.cos(2.0 * math.pi * turn_frac) * norm_scale,
        jnp.sin(2.0 * math.pi * turn_frac) * norm_scale,
    )


def dft_tables(box_edge, tile_edge):
    row_cos, row_sin = phase_parts(box_edge, tile_edge, tile_edge)
    row_table = jnp.concatenate([row_cos, -row_sin], axis=1).astype(jnp.bfloat16)
    col_cos, col_sin = phase_parts(tile_edge, box_edge, tile_edge)
    column_table = jnp.concatenate([col_cos, -col_sin], axis=0).astype(jnp.bfloat16)
    full_cos, full_sin = phase_parts(tile_edge, tile_edge, tile_edge)
    inverse_table = jnp.concatenate([full_cos, full_sin], axis=1).astype(jnp.bfloat16)
    final_table = jnp.concatenate([full_cos, -full_sin], axis=1).astype(jnp.bfloat16)
    return (row_table, column_table, inverse_table, final_table)


def project(map_slabs, slot_slab, slab_lo, slab_hi, slope_x, slope_y, first_row, row_count):
    box_edge = map_slabs.shape[2]
    center = (SLABS * SLAB_Z - 1) / 2.0
    positions = jnp.arange(box_edge, dtype=jnp.int32).astype(jnp.float32)
    row_pos = (first_row + jnp.arange(row_count, dtype=jnp.int32)).astype(jnp.float32)
    within = jnp.arange(SLAB_Z, dtype=jnp.int32)
    projection = jnp.zeros((slope_x.shape[0], row_count, box_edge), jnp.float32)
    for slot_number in range(map_slabs.shape[0]):
        slab_id = slot_slab[slot_number]
        depths = (slab_id * SLAB_Z + within).astype(jnp.float32) - center
        shift_x = slope_x[:, None] * depths[None, :]
        shift_y = slope_y[:, None] * depths[None, :]
        left_tent = tent_weight(
            positions[None, None, None, :]
            - row_pos[None, None, :, None]
            - shift_x[:, :, None, None]
        ).astype(jnp.bfloat16)
        right_tent = tent_weight(
            positions[None, None, None, :]
            - positions[None, None, :, None]
            - shift_y[:, :, None, None]
        ).astype(jnp.bfloat16)
        sheared = jnp.einsum(
            "ojax,jxy->ojay", left_tent, map_slabs[slot_number], preferred_element_type=jnp.float32
        ).astype(jnp.bfloat16)
        slab_term = jnp.einsum(
            "ojay,ojby->oab", sheared, right_tent, preferred_element_type=jnp.float32
        )
        inside = ((slab_id >= slab_lo) & (slab_id < slab_hi)).astype(jnp.float32)
        projection = projection + inside[:, None, None] * slab_term
    return projection


def finish(real_part, imag_part, spectrum_tile, inverse_table, final_table):
    edge = spectrum_tile.shape[0]
    micro_real = spectrum_tile[:, :edge].astype(jnp.float32)
    micro_imag = spectrum_tile[:, edge:].astype(jnp.float32)
    product = jnp.concatenate(
        [
            micro_real * real_part + micro_imag * imag_part,
            micro_imag * real_part - micro_real * imag_part,
        ],
        axis=0,
    ).astype(jnp.bfloat16)
    halfway = matmul(product, inverse_table)
    half_real = halfway[:edge, :edge] - halfway[edge:, edge:]
    half_imag = halfway[:edge, edge:] + halfway[edge:, :edge]
    half_stack = jnp.concatenate([half_real, half_imag], axis=0).astype(jnp.bfloat16)
    return matmul(final_table, half_stack)


def correlate(row_block, spectrum_tile, column_table, inverse_table, final_table):
    edge = spectrum_tile.shape[0]
    stacked = matmul(column_table, row_block)
    real_part = stacked[:edge, :edge] - stacked[edge:, edge:]
    imag_part = stacked[:edge, edge:] + stacked[edge:, :edge]
    return finish(real_part, imag_part, spectrum_tile, inverse_table, final_table)


def body(
    map_slabs,
    slot_slab,
    orient_index,
    slab_lo,
    slab_hi,
    tile_spectrum,
    prev_max,
    prev_sum,
    prev_sumsq,
):
    box_edge = map_slabs.shape[2]
    tile_edge = tile_spectrum.shape[1]
    orient_count = orient_index.shape[0]
    row_count = box_edge // lax.axis_size("mic")
    first_row = lax.axis_index("mic") * row_count
    slope_x, slope_y = orient_slopes(orient_index)
    partial_value = project(
        map_slabs, slot_slab, slab_lo, slab_hi, slope_x, slope_y, first_row, row_count
    )
    row_table, column_table, inverse_table, final_table = dft_tables(box_edge, tile_edge)
    local_rows = lax.psum(partial_value, "proj").astype(jnp.bfloat16)
    local_rows = jnp.einsum(
        "oay,yk->oak", local_rows, row_table, preferred_element_type=jnp.float32
    ).astype(jnp.bfloat16)
    row_spectrum = lax.all_gather(local_rows, "mic", axis=1, tiled=True)
    spectrum_tile = tile_spectrum[0]

    def per_orient(orient, running):
        best_run, total_run, square_run = running
        row_block = lax.dynamic_index_in_dim(row_spectrum, orient, 0, keepdims=False)
        scores = correlate(row_block, spectrum_tile, column_table, inverse_table, final_table)
        return (jnp.maximum(best_run, scores), total_run + scores, square_run + scores * scores)

    best_score, score_sum, score_sumsq = lax.fori_loop(
        0, orient_count, per_orient, (prev_max[0], prev_sum[0], prev_sumsq[0])
    )
    return (best_score[None], score_sum[None], score_sumsq[None])


def solution(mesh):
    in_specs = (
        P("proj", None, None, None),
        P("proj"),
        P(),
        P(),
        P(),
        P(("mic", "proj"), None, None),
        P(("mic", "proj"), None, None),
        P(("mic", "proj"), None, None),
        P(("mic", "proj"), None, None),
    )
    out_specs = (
        P(("mic", "proj"), None, None),
        P(("mic", "proj"), None, None),
        P(("mic", "proj"), None, None),
    )
    return jax.shard_map(body, mesh=mesh, in_specs=in_specs, out_specs=out_specs, check_vma=False)
```

profile of v0, /device:TPU:1, one launch (start us, length us, event | category | flops | bytes accessed | tf_op | source)
XLA Modules:
  0.0 184.0 jit_solution(656032533135612966)
XLA Ops:
  7.2 2.2 %negate_convert_fusion.2 = (bf16[256,512]{1,0:T(8,128)(2,1)S(1)}, bf16[256,512]{1,0:T(8,128)(2,1)S(1)}) fusion(), kind=kLoop, calls=%fused_computation.114 | loop fusion | flops 2490368 | bytes 524288 | tf_op jit(solution)/shard_map/convert.11
  14.9 3.8 %and_convert_fusion = (f32[4]{0:T(128)S(1)}, f32[4]{0:T(128)S(1)}, f32[4]{0:T(128)S(1)}, f32[4]{0:T(128)S(1)}, f32[4]{0:T(128)S(1)}) fusion(s32[4]{0:T(128)} %param.15, s32[4]{0:T(128)} %param.14, s32[]{:T(128)} %bitcast.31, s32[]{:T(128)} %bitcast.19, s32[]{:T(128)} %bitcast.13, s32[]{:T(128)} %bitcast.7, s32[]{:T(128)} %bitcast.25), kind=kLoop, calls=%fused_computation.133 | loop fusion | flops 80 | bytes 132 | tf_op jit(solution)/shard_map/convert_element_type | solution.py:84
  18.8 9.3 %maximum_convert_fusion = (bf16[4,8,256,256]{3,2,1,0:T(8,128)(2,1)}, bf16[4,8,256,256]{3,2,1,0:T(8,128)(2,1)}, bf16[4,8,256,256]{3,2,1,0:T(8,128)(2,1)}, bf16[4,...) fusion(f32[4,8]{1,0:T(4,128)S(1)} %get-tuple-element.217, f32[256,256]{1,0:T(8,128)S(1)} %broadcast_subtract_fusion, ...), kind=kLoop, calls=%fused_computation.29 | loop fusion | flops 52428800 | bytes 21234304 | tf_op jit(solution)/shard_map/convert_element_type | solution.py:77
  28.4 3.8 %fusion.72 = f32[4,4,256]{2,1,0:T(4,128)S(1)} fusion(bf16[4,8,256,256]{3,2,1,0:T(8,128)(2,1)} %get-tuple-element.203, bf16[5,8,256,256]{3,2,1,0:T(8,128)(2,1)} %param.11, bf16[4,8,4,256]{3,2,1,0:T(4,128)(2,1)S(1)} %get-tuple-element.208, f32[4]{0:T(128)S(1)} %get-tuple-element.212), kind=kOutput, calls=%fused_computation.73 | convolution fusion | flops 33591296 | bytes 5324816 | tf_op jit(solution)/shard_map/ojay,ojby->oab/dot_general | solution.py:81
  32.2 3.8 %fusion.69 = f32[4,4,256]{2,1,0:T(4,128)S(1)} fusion(f32[4,4,256]{2,1,0:T(4,128)S(1)} %fusion.72, bf16[4,8,256,256]{3,2,1,0:T(8,128)(2,1)} %get-tuple-element.200, bf16[5,8,256,256]{3,2,1,0:T(8,128)(2,1)} %param.11, bf16[4,8,4,256]{3,2,1,0:T(4,128)(2,1)S(1)} %get-tuple-element.205, f32[4]{0:T(128)S(1)} %get-tuple-element.211), kind=kOutput, calls=%fused_computation.72 | convolution fusion | flops 33595392 | bytes 5341200 | tf_op jit(solution)/shard_map/ojay,ojby->oab/dot_general | solution.py:81
  36.1 3.8 %fusion.63 = f32[4,4,256]{2,1,0:T(4,128)S(1)} fusion(f32[4,4,256]{2,1,0:T(4,128)S(1)} %fusion.69, bf16[4,8,256,256]{3,2,1,0:T(8,128)(2,1)} %get-tuple-element.201, bf16[5,8,256,256]{3,2,1,0:T(8,128)(2,1)} %param.11, bf16[4,8,4,256]{3,2,1,0:T(4,128)(2,1)S(1)} %get-tuple-element.206, f32[4]{0:T(128)S(1)} %get-tuple-element.210), kind=kOutput, calls=%fused_computation.70 | convolution fusion | flops 33595392 | bytes 5341200 | tf_op jit(solution)/shard_map/ojay,ojby->oab/dot_general | solution.py:81
  39.9 3.8 %fusion.57 = f32[4,4,256]{2,1,0:T(4,128)S(1)} fusion(f32[4,4,256]{2,1,0:T(4,128)S(1)} %fusion.63, bf16[4,8,256,256]{3,2,1,0:T(8,128)(2,1)} %get-tuple-element.202, bf16[5,8,256,256]{3,2,1,0:T(8,128)(2,1)} %param.11, bf16[4,8,4,256]{3,2,1,0:T(4,128)(2,1)S(1)} %get-tuple-element.207, f32[4]{0:T(128)S(1)} %get-tuple-element.213), kind=kOutput, calls=%fused_computation.68 | convolution fusion | flops 33595392 | bytes 5341200 | tf_op jit(solution)/shard_map/ojay,ojby->oab/dot_general | solution.py:81
  43.8 3.9 %fusion.51 = f32[4,4,256]{2,1,0:T(4,128)S(1)} fusion(f32[4,4,256]{2,1,0:T(4,128)S(1)} %fusion.57, bf16[4,8,256,256]{3,2,1,0:T(8,128)(2,1)} %get-tuple-element.199, bf16[5,8,256,256]{3,2,1,0:T(8,128)(2,1)} %param.11, bf16[4,8,4,256]{3,2,1,0:T(4,128)(2,1)S(1)} %get-tuple-element.204, f32[4]{0:T(128)S(1)} %get-tuple-element.209), kind=kOutput, calls=%fused_computation.66 | convolution fusion | flops 33595392 | bytes 5341200 | tf_op jit(solution)/shard_map/ojay,ojby->oab/dot_general | solution.py:81
  47.7 11.2 %psum.7 = bf16[4,4,256]{2,1,0:T(4,128)(2,1)S(1)} all-reduce(f32[4,4,256]{2,1,0:T(4,128)S(1)} %fusion.51), channel_id=1, replica_groups=mesh['mic'=64,'proj'=4] {'proj'}, use_global_device_ids=true, to_apply=%region_0.1 | all-reduce | flops 4096 | bytes 24576 | tf_op jit(solution)/shard_map/psum | solution.py:136
  63.3 4.0 %fusion.101 = bf16[512,512]{1,0:T(8,128)(2,1)S(1)} fusion(), kind=kLoop, calls=%fused_computation.93 | loop fusion | flops 4194304 | bytes 524288 | tf_op jit(solution)/shard_map/convert.7
  67.3 2.2 %negate_convert_fusion.1 = (bf16[512,256]{1,0:T(8,128)(2,1)S(1)}, bf16[512,256]{1,0:T(8,128)(2,1)S(1)}) fusion(), kind=kLoop, calls=%fused_computation.110 | loop fusion | flops 2490368 | bytes 524288 | tf_op jit(solution)/shard_map/convert.9
  70.3 4.4 %negate_convert_fusion = (bf16[512,512]{1,0:T(8,128)(2,1)S(1)}, bf16[512,512]{1,0:T(8,128)(2,1)S(1)}) fusion(), kind=kLoop, calls=%fused_computation.82 | loop fusion | flops 4980736 | bytes 1048576 | tf_op jit(solution)/shard_map/convert.5
  74.7 1.6 pad_maximum_fusion
  76.3 64.2 %all-gather.2.cloned.1.call-done = bf16[4,256,1024]{2,0,1:T(4,128)(2,1)} async-done(((bf16[4,4,1024]{2,0,1:T(4,128)(2,1)}), bf16[4,256,1024]{2,0,1:T(4,128)(2,1)}) %all-gather.2.cloned.1.call-update) | async-done | bytes 2097168 | tf_op jit(solution)/shard_map/all_gather | solution.py:140
  140.5 3.6 %copy.22 = bf16[4,256,1024]{2,1,0:T(8,128)(2,1)} copy(bf16[4,256,1024]{2,0,1:T(4,128)(2,1)} %all-gather.2.cloned.1.call-done) | data formatting | bytes 4194304 | tf_op jit(solution)/shard_map/while | solution.py:149
  144.0 29.2 %while.17 = (s32[]{:T(128)}, f32[512,512]{0,1:T(8,128)S(1)}, f32[512,512]{0,1:T(8,128)S(1)}, f32[512,512]{0,1:T(8,128)S(1)}, bf16[512,1024]{1,0:T(8,128)(2,1)}, ...) while((s32[]{:T(128)}, f32[512,512]{0,1:T(8,128)S(1)}, ...), condition=%wide.region_2.3_spmd, body=%wide.region_1.2_spmd.sunk | while | flops 2156920832 | bytes 44040888 | solution.py:149
  144.0 2.0 %convolution_bitcast_fusion.3 = f32[1024,1024]{1,0:T(8,128)S(1)} fusion(bf16[1024,256]{1,0:T(8,128)(2,1)} %get-tuple-element.336, bf16[4,256,1024]{2,1,0:T(8,128)(2,1)} %get-tuple-element.335, s32[]{:T(128)} %get-tuple-element.320), kind=kOutput, calls=%fused_computation.clone.1 | convolution fusion | flops 536870912 | bytes 5243392 | tf_op jit(solution)/shard_map/while/body/eval_jaxpr/dot_general | solution.py:18
  149.7 1.6 multiply_add_fusion.2
  151.3 2.0 %convolution_bitcast_fusion.3 = f32[1024,1024]{1,0:T(8,128)S(1)} fusion(bf16[1024,256]{1,0:T(8,128)(2,1)} %get-tuple-element.336, bf16[4,256,1024]{2,1,0:T(8,128)(2,1)} %get-tuple-element.335, s32[]{:T(128)} %get-tuple-element.320), kind=kOutput, calls=%fused_computation.clone.1 | convolution fusion | flops 536870912 | bytes 5243392 | tf_op jit(solution)/shard_map/while/body/eval_jaxpr/dot_general | solution.py:18
  157.1 1.6 multiply_add_fusion.2
  158.7 2.0 %convolution_bitcast_fusion.3 = f32[1024,1024]{1,0:T(8,128)S(1)} fusion(bf16[1024,256]{1,0:T(8,128)(2,1)} %get-tuple-element.336, bf16[4,256,1024]{2,1,0:T(8,128)(2,1)} %get-tuple-element.335, s32[]{:T(128)} %get-tuple-element.320), kind=kOutput, calls=%fused_computation.clone.1 | convolution fusion | flops 536870912 | bytes 5243392 | tf_op jit(solution)/shard_map/while/body/eval_jaxpr/dot_general | solution.py:18
  164.4 1.6 multiply_add_fusion.2
  166.0 2.0 %convolution_bitcast_fusion.3 = f32[1024,1024]{1,0:T(8,128)S(1)} fusion(bf16[1024,256]{1,0:T(8,128)(2,1)} %get-tuple-element.336, bf16[4,256,1024]{2,1,0:T(8,128)(2,1)} %get-tuple-element.335, s32[]{:T(128)} %get-tuple-element.320), kind=kOutput, calls=%fused_computation.clone.1 | convolution fusion | flops 536870912 | bytes 5243392 | tf_op jit(solution)/shard_map/while/body/eval_jaxpr/dot_general | solution.py:18
  171.7 1.6 multiply_add_fusion.2
  (60 shorter events, 26.5 us)
Async XLA Ops:
  7.2 133.3 %all-gather.2.cloned.1.call-start = ((), (), s32[]{:S(2)}) async-start(), calls=%async_computation | async-start | bytes 2129920 | tf_op jit(solution)/shard_map/all_gather | solution.py:140
  43.8 16.0 %copy-start.3 = (f32[1,512,512]{2,1,0:T(8,128)S(1)}, f32[1,512,512]{2,1,0:T(8,128)}, u32[]{:S(2)}) copy-start(f32[1,512,512]{2,1,0:T(8,128)} %param.17) | copy-start | bytes 3145732
  144.0 2.0 %copy-start.1 = (bf16[512,1024]{1,0:T(8,128)(2,1)S(1)}, bf16[512,1024]{1,0:T(8,128)(2,1)}, u32[]{:S(2)}) copy-start(bf16[512,1024]{1,0:T(8,128)(2,1)} %get-tuple-element.334) | copy-start | bytes 3145732 | tf_op jit(solution)/shard_map/while
  146.0 1.2 copy-start.2
  148.5 1.2 copy-start
  151.3 2.0 %copy-start.1 = (bf16[512,1024]{1,0:T(8,128)(2,1)S(1)}, bf16[512,1024]{1,0:T(8,128)(2,1)}, u32[]{:S(2)}) copy-start(bf16[512,1024]{1,0:T(8,128)(2,1)} %get-tuple-element.334) | copy-start | bytes 3145732 | tf_op jit(solution)/shard_map/while
  153.3 1.2 copy-start.2
  155.8 1.2 copy-start
  158.6 2.0 %copy-start.1 = (bf16[512,1024]{1,0:T(8,128)(2,1)S(1)}, bf16[512,1024]{1,0:T(8,128)(2,1)}, u32[]{:S(2)}) copy-start(bf16[512,1024]{1,0:T(8,128)(2,1)} %get-tuple-element.334) | copy-start | bytes 3145732 | tf_op jit(solution)/shard_map/while
  160.7 1.2 copy-start.2
  163.1 1.2 copy-start
  165.9 2.0 %copy-start.1 = (bf16[512,1024]{1,0:T(8,128)(2,1)S(1)}, bf16[512,1024]{1,0:T(8,128)(2,1)}, u32[]{:S(2)}) copy-start(bf16[512,1024]{1,0:T(8,128)(2,1)} %get-tuple-element.334) | copy-start | bytes 3145732 | tf_op jit(solution)/shard_map/while
  168.0 1.2 copy-start.2
  170.4 1.2 copy-start
Sparse Core Ops, SparseCore 0:
  59.9 80.5 all-gather.1
where the time goes:
time: 186 us; the launch traced here: 184 us
  waiting for transfers between devices  64.2 us (35%)
  matrix products  38.7 us (21%)
  other arithmetic  33.8 us (18%)
  local copies, waits for them, and re-layouts  18.5 us (10%)
  between operations  17.3 us (9%)
  blocking collectives  11.2 us (6%)
    all_gather x1, waiting for transfers between devices, body(): row_spectrum = lax.all_gather(local_rows, 'mic', axis=1, tiled=True)  64.2 us
    dot_general x5, matrix products, project(): jnp.einsum('ojay,ojby->oab', sheared, right_tent, preferred_element_type=...  19.3 us
    dot_general x12, matrix products, matmul(): return jnp.dot(left_op, right_op, preferred_element_type=jnp.float32)  19.2 us
    another operation x12, other arithmetic  17 us
    psum x1, blocking collectives, body(): local_rows = lax.psum(partial_value, 'proj').astype(jnp.bfloat16)  11.2 us
    convert_element_type x1, other arithmetic, project(): right_tent = tent_weight(positions[None, None, None, :] - positions[None,...  9.32 us
    while x4, local copies, waits for them, and re-layouts, body(): lax.fori_loop(0, orient_count, per_orient, (prev_max[0], prev_sum[0], pre...  7.48 us
    while x24, local copies, waits for them, and re-layouts  5.51 us
  transfers between devices with their start and end apart: 1, of which 1 were waited for; matrix products, arithmetic and copies ran while one was open for 9% of the time, Pallas kernels for 0%

commit v1 on v0

v1 whole, which is shorter than its diff:
```python
import functools
import math

import jax
import jax.numpy as jnp
import ml_dtypes
import numpy as np
from jax import lax
from jax.experimental import pallas as pl
from jax.experimental.pallas import tpu as pltpu
from jax.sharding import PartitionSpec as P

MESH = pl.DeviceIdType.MESH
SLAB_Z = 8
SLABS = 12
NORI = 256
BOX = 256
TILE = 512
ORI = 4
SLOTS = 5
HALF = BOX // 2
ROWS = 272
GOLDEN = 2.399963
MAX_SLOPE = 0.5


def turns(freqs, pixels):
    angle = 2.0 * np.pi * ((freqs[:, None] * pixels[None, :]) % TILE) / TILE
    return np.cos(angle) / math.sqrt(TILE), np.sin(angle) / math.sqrt(TILE)


def bf16(array):
    return np.asarray(array, np.float32).astype(ml_dtypes.bfloat16)


@functools.lru_cache(maxsize=None)
def tables():
    evens, odds = np.arange(0, BOX, 2), np.arange(1, BOX, 2)
    freq = np.concatenate([evens, odds])
    all_freq = np.concatenate([freq, [BOX]])
    cos, sin = turns(all_freq, np.arange(BOX))
    column = np.zeros((2 * ROWS, BOX))
    column[: BOX + 1] = cos
    column[ROWS : ROWS + BOX + 1] = -sin
    spread = []
    for pixels in (evens, odds):
        parts = []
        for freqs in (evens, odds):
            cos, sin = turns(pixels, freqs)
            parts.append(np.block([[cos, -sin], [sin, cos]]))
        spread.append(np.concatenate(parts, axis=1))
    inverse = []
    for freqs in (evens, odds):
        cos, sin = turns(np.concatenate([freqs, freqs + BOX]), np.arange(BOX))
        inverse.append(np.block([[cos, sin], [-sin, cos]]))
    final = []
    for freqs in (evens, odds):
        cos, sin = turns(np.arange(BOX), freqs)
        final.append(np.concatenate([cos, -sin], axis=1))
    final[0][:, 0] *= 0.5
    final[0][:, HALF] = 0.5 * turns(np.arange(BOX), np.array([BOX]))[0][:, 0]
    return tuple(
        bf16(t)
        for t in (
            column,
            np.stack(spread),
            np.stack(inverse),
            np.stack(final),
        )
    )


def dot(a, b):
    return jnp.dot(a, b, preferred_element_type=jnp.float32)


def fill_selections(rowsel, colsel):
    one_hot = lambda mask: jnp.where(mask, 1.0, 0.0).astype(jnp.bfloat16)
    lane = lax.broadcasted_iota(jnp.int32, (ROWS, 128), 1)
    row = lax.broadcasted_iota(jnp.int32, (ROWS, 128), 0)
    freq = jnp.where(row < 128, 2 * row, jnp.where(row <= BOX, 2 * row - 255, -1))
    freq = jnp.where(row == BOX, BOX, freq)
    mirror = jnp.where(freq <= 0, freq, TILE - freq)
    for block in range(4):
        lanes = slice(block * 128, (block + 1) * 128)
        rowsel[:ROWS, lanes] = one_hot(lane + block * 128 == freq)
        rowsel[ROWS:, lanes] = one_hot(lane + block * 128 == mirror)
    twice = 2 * lax.broadcasted_iota(jnp.int32, (TILE, 128), 1)
    source = lax.broadcasted_iota(jnp.int32, (TILE, 128), 0)
    for block, offset in enumerate((0, 1, BOX, BOX + 1)):
        lanes = slice(block * 128, (block + 1) * 128)
        colsel[:TILE, lanes] = one_hot(source - twice == offset)
        colsel[TILE:, lanes] = one_hot((source + twice + offset) % TILE == 0)


def project_kernel(
    orient_ref,
    slot_ref,
    lo_ref,
    hi_ref,
    map_ref,
    tile_ref,
    template_ref,
    folded_ref,
    slabs,
    tile,
    rowsel,
    colsel,
    left,
    right,
    sheared,
    acc,
    sib_recv,
    z_send,
    z_recv,
    template,
    picked,
    folded,
    in_sem,
    slab_sem,
    out_sem,
    send_sem,
    recv_sem,
):
    mic, proj = lax.axis_index("mic"), lax.axis_index("proj")
    x, z_hi, y = mic // 16, (mic // 4) % 4, mic % 4
    z_lo, core = proj // 2, proj % 2
    own = (x + y) % 4

    def device(dx, dy, which_z, which_core):
        chip = (((x + dx + 4) % 4) * 4 + z_hi) * 4 + (y + dy + 4) % 4
        return (chip, which_z * 2 + which_core)

    sibling = device(0, 0, z_lo, 1 - core)
    across = device(0, 0, 1 - z_lo, core)
    along = [(1 - core, core), (core - 1, -core), (1 - 2 * core, 1 - 2 * core)]
    targets = [device(dx, dy, z_lo, c) for dx, dy in along for c in (0, 1)]
    sources = [
        device(1, 0, z_lo, 0),
        device(-1, 0, z_lo, 0),
        device(-1, -1, z_lo, 0),
        device(0, 1, z_lo, 1),
        device(0, -1, z_lo, 1),
        device(1, 1, z_lo, 1),
    ]

    barrier = pltpu.get_barrier_semaphore()
    for peer in [sibling, across] + sources:
        pl.semaphore_signal(barrier, inc=1, device_id=peer, device_id_type=MESH)

    for slot in range(SLOTS):
        pltpu.make_async_copy(map_ref.at[slot], slabs.at[slot], slab_sem.at[slot]).start()
    loads = [
        pltpu.make_async_copy(src, dst, in_sem.at[i])
        for i, (src, dst) in enumerate(((tile_ref.at[0], tile),))
    ]
    for load in loads:
        load.start()

    fill_selections(rowsel, colsel)

    step = jnp.full((SLAB_Z, 128), orient_ref[own]).astype(jnp.float32)
    radius = MAX_SLOPE * jnp.sqrt((step + 0.5) / NORI)
    slope_x = radius * jnp.cos(GOLDEN * step)
    slope_y = radius * jnp.sin(GOLDEN * step)
    within = lax.broadcasted_iota(jnp.int32, (SLAB_Z, 128), 0)
    center = (SLABS * SLAB_Z - 1) / 2.0

    def taps(shift, weight):
        low = jnp.floor(shift)
        first = jnp.maximum(0.0, 1.0 - jnp.abs(low - shift)) * weight
        second = jnp.maximum(0.0, 1.0 - jnp.abs((low + 1.0) - shift)) * weight
        return low, first, second

    left_gap = (
        lax.broadcasted_iota(jnp.int32, (160, 128), 1) - lax.broadcasted_iota(jnp.int32, (160, 128), 0)
    ).astype(jnp.float32).astype(jnp.bfloat16)
    right_gap = (
        lax.broadcasted_iota(jnp.int32, (BOX, 128), 0) - 2 * lax.broadcasted_iota(jnp.int32, (BOX, 128), 1)
    ).astype(jnp.float32).astype(jnp.bfloat16)
    zero = jnp.zeros((), jnp.bfloat16)
    for j in range(SLAB_Z):
        left[j, 160:, :128] = jnp.zeros((96, 128), jnp.bfloat16)
        left[j, :96, 128:] = jnp.zeros((96, 128), jnp.bfloat16)
    acc[...] = jnp.zeros_like(acc)

    def one_slot(slot, carry):
        slab = jnp.full((SLAB_Z, 128), slot_ref[slot])
        depth = (slab * SLAB_Z + within).astype(jnp.float32) - center
        inside = jnp.where((slab >= lo_ref[own]) & (slab < hi_ref[own]), 1.0, 0.0)
        nx, x0, x1 = taps(slope_x * depth, inside)
        ny, y0, y1 = taps(slope_y * depth, 1.0)
        for j in range(SLAB_Z):
            row = lambda v, shape: jnp.broadcast_to(v[j : j + 1].astype(jnp.bfloat16), shape)
            w0, w1 = row(x0, (160, 128)), row(x1, (160, 128))
            for first, lanes, offset in ((0, 0, 0.0), (96, 128, 32.0)):
                block = jnp.where(
                    left_gap == row(nx - offset, (160, 128)),
                    w0,
                    jnp.where(left_gap == row(nx + 1.0 - offset, (160, 128)), w1, zero),
                )
                left[j, first : first + 160, lanes : lanes + 128] = block
            w0, w1 = row(y0, (BOX, 128)), row(y1, (BOX, 128))
            at0, at1, at2 = (right_gap == row(ny + k, (BOX, 128)) for k in (0.0, 1.0, 2.0))
            right[j * BOX : (j + 1) * BOX, :128] = jnp.where(at0, w0, jnp.where(at1, w1, zero))
            right[j * BOX : (j + 1) * BOX, 128:] = jnp.where(at1, w0, jnp.where(at2, w1, zero))
        pltpu.make_async_copy(map_ref.at[slot], slabs.at[slot], slab_sem.at[slot]).wait()
        for j in range(SLAB_Z):
            sheared[:, j * BOX : (j + 1) * BOX] = dot(left[j], slabs[slot, j]).astype(jnp.bfloat16)
        acc[...] += dot(sheared[...], right[...])
        return carry

    lax.fori_loop(0, SLOTS, one_slot, 0)

    def send(i, arrival, src, dst, peer):
        return pltpu.make_async_remote_copy(
            src_ref=src,
            dst_ref=dst,
            send_sem=send_sem.at[i],
            recv_sem=recv_sem.at[arrival],
            device_id=peer,
            device_id_type=MESH,
        )

    mine = pl.ds(pl.multiple_of(core * HALF, HALF), HALF)
    theirs = pl.ds(pl.multiple_of((1 - core) * HALF, HALF), HALF)
    pl.semaphore_wait(barrier, 8)
    hop = send(0, 0, acc.at[theirs], sib_recv, sibling)
    hop.start()
    for load in loads:
        load.wait()
    rows = dot(rowsel[...], tile[...])
    picked[:ROWS, :TILE] = rows[:ROWS, :TILE].astype(jnp.bfloat16)
    picked[:ROWS, TILE:] = rows[ROWS:, :TILE].astype(jnp.bfloat16)
    picked[ROWS:, :TILE] = rows[:ROWS, TILE:].astype(jnp.bfloat16)
    picked[ROWS:, TILE:] = (-rows[ROWS:, TILE:]).astype(jnp.bfloat16)
    hop.wait()
    chip_sum = acc[mine, :] + sib_recv[...]
    z_send[...] = chip_sum.astype(jnp.bfloat16)
    hop = send(1, 1, z_send, z_recv, across)
    hop.start()
    folded[...] = dot(picked[...], colsel[...])
    save = pltpu.make_async_copy(folded, folded_ref, out_sem.at[0])
    save.start()
    hop.wait()
    template[own, mine, :] = (chip_sum + z_recv[...].astype(jnp.float32)).astype(jnp.bfloat16)
    block = template.at[own, mine]
    hops = [send(3 + i, 3 + core * 3 + i // 2, block, block, peer) for i, peer in enumerate(targets)]
    hops.append(send(2, 2, block, block, sibling))
    for hop in hops:
        hop.start()
    arrivals = [(2, own, 1 - core)]
    for source_core in range(2):
        for i, offset in enumerate((3, 1, 2)):
            arrivals.append((3 + source_core * 3 + i, (own + offset) % 4, source_core))
    for arrival, orient, source_core in arrivals:
        landed = template.at[orient, pl.ds(pl.multiple_of(source_core * HALF, HALF), HALF)]
        send(2, arrival, landed, landed, sibling).wait_recv()
    for hop in hops:
        hop.wait_send()
    out = pltpu.make_async_copy(template, template_ref, out_sem.at[1])
    out.start()
    out.wait()
    save.wait()


def correlate_kernel(
    template_ref,
    folded_ref,
    column_ref,
    spread_ref,
    inverse_ref,
    final_ref,
    max_ref,
    sum_ref,
    sumsq_ref,
    out_max_ref,
    out_sum_ref,
    out_sumsq_ref,
    template,
    folded,
    column,
    spread,
    inverse,
    final,
    best,
    total,
    square,
    cs,
    prod,
    half,
    even_part,
    odd_part,
    in_sem,
    out_sem,
):
    copies = [
        pltpu.make_async_copy(src, dst, in_sem.at[i])
        for i, (src, dst) in enumerate(
            (
                (template_ref, template),
                (column_ref, column),
                (spread_ref, spread),
                (folded_ref, folded),
                (inverse_ref, inverse),
                (final_ref, final),
                (max_ref.at[0], best),
                (sum_ref.at[0], total),
                (sumsq_ref.at[0], square),
            )
        )
    ]
    for copy in copies:
        copy.start()
    copies[0].wait()
    copies[1].wait()
    for o in range(ORI):
        value = dot(column[...], template[o]).astype(jnp.bfloat16)
        cs[o, :, 0:128] = value[:ROWS, :128]
        cs[o, :, 128:256] = value[ROWS:, :128]
        cs[o, :, 256:384] = value[:ROWS, 128:]
        cs[o, :, 384:512] = value[ROWS:, 128:]
    copies[2].wait()
    copies[3].wait()
    for o in range(ORI):
        for q in range(2):
            even = dot(cs[o, :, :256], spread[0, :, q * 256 : (q + 1) * 256])
            odd = dot(cs[o, :, 256:], spread[1, :, q * 256 : (q + 1) * 256])
            for h, spec in enumerate((even + odd, even - odd)):
                lanes = slice((2 * h + q) * 128, (2 * h + q + 1) * 128)
                t_re, t_im = folded[:ROWS, lanes], folded[ROWS:, lanes]
                s_re, s_im = spec[:, :128], spec[:, 128:]
                re = t_re * s_re + t_im * s_im
                im = t_im * s_re - t_re * s_im
                prod[o, q, 8:, h * 128 : (h + 1) * 128] = re[8:BOX].astype(jnp.bfloat16)
                prod[o, q, 8:, 256 + h * 128 : 256 + (h + 1) * 128] = im[8:BOX].astype(jnp.bfloat16)
                top_re = re[:8] - im[BOX : BOX + 8]
                top_im = im[:8] + re[BOX : BOX + 8]
                prod[o, q, :8, h * 128 : (h + 1) * 128] = top_re.astype(jnp.bfloat16)
                prod[o, q, :8, 256 + h * 128 : 256 + (h + 1) * 128] = top_im.astype(jnp.bfloat16)
    copies[4].wait()
    for o in range(ORI):
        even = dot(prod[o, 0], inverse[0])
        odd = dot(prod[o, 1], inverse[1])
        low, high = (even + odd).astype(jnp.bfloat16), (even - odd).astype(jnp.bfloat16)
        for parity in range(2):
            rows = slice(parity * 128, (parity + 1) * 128)
            half[o, parity, :128, :256] = low[rows, :256]
            half[o, parity, 128:, :256] = low[rows, 256:]
            half[o, parity, :128, 256:] = high[rows, :256]
            half[o, parity, 128:, 256:] = high[rows, 256:]
    for copy in copies[5:]:
        copy.wait()
    outs = []
    for block in range(2):
        lanes = slice(block * 256, (block + 1) * 256)
        for o in range(ORI):
            even_part[o] = dot(final[0], half[o, 0, :, lanes])
            odd_part[o] = dot(final[1], half[o, 1, :, lanes])

        def combine(i, carry):
            rows = pl.ds(pl.multiple_of(i * 16, 16), 16)
            high_rows = pl.ds(pl.multiple_of(i * 16 + BOX, 16), 16)
            for sign, dest in ((1, rows), (-1, high_rows)):
                peak, run, energy = best[dest, lanes], total[dest, lanes], square[dest, lanes]
                for o in range(ORI):
                    even, odd = even_part[o, rows, :], odd_part[o, rows, :]
                    score = even + odd if sign == 1 else even - odd
                    peak, run, energy = jnp.maximum(peak, score), run + score, energy + score * score
                best[dest, lanes], total[dest, lanes], square[dest, lanes] = peak, run, energy
            return carry

        lax.fori_loop(0, BOX // 16, combine, 0)
        for i, (src, dst) in enumerate(((best, out_max_ref), (total, out_sum_ref), (square, out_sumsq_ref))):
            copy = pltpu.make_async_copy(src.at[:, lanes], dst.at[0, :, lanes], out_sem.at[block * 3 + i])
            copy.start()
            outs.append(copy)
    for copy in outs:
        copy.wait()


def body(map_slabs, slot_slab, orient_index, slab_lo, slab_hi, tile_spectrum, prev_max, prev_sum, prev_sumsq):
    column, spread, inverse, final = (jnp.asarray(t) for t in tables())
    smem = pl.BlockSpec(memory_space=pltpu.SMEM)
    hbm = pl.BlockSpec(memory_space=pl.ANY)
    vmem = pltpu.VMEM
    template, folded = pl.pallas_call(
        project_kernel,
        name="project",
        out_shape=(
            jax.ShapeDtypeStruct((ORI, BOX, BOX), jnp.bfloat16),
            jax.ShapeDtypeStruct((2 * ROWS, TILE), jnp.float32),
        ),
        in_specs=[smem] * 4 + [hbm] * 2,
        out_specs=(hbm, hbm),
        scratch_shapes=[
            vmem((SLOTS, SLAB_Z, BOX, BOX), jnp.bfloat16),
            vmem((TILE, 2 * TILE), jnp.bfloat16),
            vmem((2 * ROWS, TILE), jnp.bfloat16),
            vmem((2 * TILE, TILE), jnp.bfloat16),
            vmem((SLAB_Z, BOX, BOX), jnp.bfloat16),
            vmem((SLAB_Z * BOX, BOX), jnp.bfloat16),
            vmem((BOX, SLAB_Z * BOX), jnp.bfloat16),
            vmem((BOX, BOX), jnp.float32),
            vmem((HALF, BOX), jnp.float32),
            vmem((HALF, BOX), jnp.bfloat16),
            vmem((HALF, BOX), jnp.bfloat16),
            vmem((ORI, BOX, BOX), jnp.bfloat16),
            vmem((2 * ROWS, 2 * TILE), jnp.bfloat16),
            vmem((2 * ROWS, TILE), jnp.float32),
            pltpu.SemaphoreType.DMA((1,)),
            pltpu.SemaphoreType.DMA((SLOTS,)),
            pltpu.SemaphoreType.DMA((2,)),
            pltpu.SemaphoreType.DMA((9,)),
            pltpu.SemaphoreType.DMA((9,)),
        ],
        compiler_params=pltpu.CompilerParams(
            collective_id=0, has_side_effects=True, vmem_limit_bytes=40 << 20
        ),
    )(orient_index, slot_slab, slab_lo, slab_hi, map_slabs, tile_spectrum)
    plane = jax.ShapeDtypeStruct((1, TILE, TILE), jnp.float32)
    return pl.pallas_call(
        correlate_kernel,
        name="correlate",
        out_shape=(plane, plane, plane),
        in_specs=[hbm] * 9,
        out_specs=(hbm, hbm, hbm),
        scratch_shapes=[
            vmem((ORI, BOX, BOX), jnp.bfloat16),
            vmem((2 * ROWS, TILE), jnp.float32),
            vmem((2 * ROWS, BOX), jnp.bfloat16),
            vmem((2, BOX, TILE), jnp.bfloat16),
            vmem((2, TILE, TILE), jnp.bfloat16),
            vmem((2, BOX, BOX), jnp.bfloat16),
            vmem((TILE, TILE), jnp.float32),
            vmem((TILE, TILE), jnp.float32),
            vmem((TILE, TILE), jnp.float32),
            vmem((ORI, ROWS, TILE), jnp.bfloat16),
            vmem((ORI, 2, BOX, TILE), jnp.bfloat16),
            vmem((ORI, 2, BOX, TILE), jnp.bfloat16),
            vmem((ORI, BOX, BOX), jnp.float32),
            vmem((ORI, BOX, BOX), jnp.float32),
            pltpu.SemaphoreType.DMA((9,)),
            pltpu.SemaphoreType.DMA((6,)),
        ],
        compiler_params=pltpu.CompilerParams(vmem_limit_bytes=40 << 20),
    )(template, folded, column, spread, inverse, final, prev_max, prev_sum, prev_sumsq)


def solution(mesh):
    tile_spec = P(("mic", "proj"), None, None)
    return jax.shard_map(
        body,
        mesh=mesh,
        in_specs=(P("proj", None, None, None), P("proj"), P(), P(), P(), tile_spec, tile_spec, tile_spec, tile_spec),
        out_specs=(tile_spec, tile_spec, tile_spec),
        check_vma=False,
    )
```

time: 186 us -> 38 us (0.20)
  waiting for transfers between devices: 64.2 us -> 0 us
  matrix products: 38.7 us -> 0 us
  other arithmetic: 33.8 us -> 0 us
  Pallas kernels: 0 us -> 30.7 us
  between operations: 17.3 us -> 0.74 us
  local copies, waits for them, and re-layouts: 18.5 us -> 6.36 us
  blocking collectives: 11.2 us -> 0 us
    all_gather x1 -> x0, waiting for transfers between devices: 64.2 us -> none  [body(): row_spectrum = lax.all_gather(local_rows, 'mic', axis=1, tiled=True)]
    dot_general x18 -> x0, matrix products: 38.7 us -> none  [the longest x5 19.3 us: project(): jnp.einsum('ojay,ojby->oab', sheared, right_tent, preferred_element_type=...]
    pallas_call x0 -> x2, Pallas kernels: none -> 30.7 us  [the longest x1 24.3 us: body(): pl.pallas_call(project_kernel, name='project', out_shape=(jax.ShapeDtypeS...]
    another operation x12 -> x0, other arithmetic: 17 us -> none
    convert_element_type x5 -> x0, other arithmetic: 13.4 us -> none  [the longest x1 9.32 us: project(): right_tent = tent_weight(positions[None, None, None, :] - positions[None,...]
    while x28 -> x0, local copies, waits for them, and re-layouts: 13 us -> none  [the longest x4 7.48 us: body(): lax.fori_loop(0, orient_count, per_orient, (prev_max[0], prev_sum[0], pre...]
    psum x1 -> x0, blocking collectives: 11.2 us -> none  [body(): local_rows = lax.psum(partial_value, 'proj').astype(jnp.bfloat16)]
    unnamed x5 -> x26, local copies, waits for them, and re-layouts: 3.45 us -> 6.36 us
  transfers between devices with their start and end apart: 1 -> 0, of which waited for: 1 -> 0; matrix products, arithmetic and copies ran while one was open for 9% -> 0% of each run, Pallas kernels for 0% -> 0%
where the time goes in v1:
time: 38 us; the launch traced here: 37.8 us
  Pallas kernels  30.7 us (81%)
  local copies, waits for them, and re-layouts  6.36 us (17%)
  between operations  0.74 us (2%)
    pallas_call x1, Pallas kernels, body(): pl.pallas_call(project_kernel, name='project', out_shape=(jax.ShapeDtypeS...  24.3 us
    pallas_call x1, Pallas kernels, body(): pl.pallas_call(correlate_kernel, name='correlate', out_shape=(plane, plan...  6.37 us
    unnamed x26, local copies, waits for them, and re-layouts  6.36 us

profile of v1, /device:TPU:1, one launch (start us, length us, event | category | flops | bytes accessed | tf_op | source)
XLA Modules:
  0.0 37.8 jit_solution(5502340881941590873)
XLA Ops:
  0.6 0.0 copy-start
  0.6 2.5 %copy-done = bf16[5,8,256,256]{3,2,1,0:T(8,128)(2,1)S(1)} copy-done((bf16[5,8,256,256]{3,2,1,0:T(8,128)(2,1)S(1)}, bf16[5,8,256,256]{3,2,1,0:T(8,128)(2,1)}, u32[]{:S(2)}) %copy-start) | copy-done | bytes 5242904
  3.1 0.0 copy-start.1
  3.1 1.2 %copy-done.1 = bf16[1,512,1024]{2,1,0:T(8,128)(2,1)S(1)} copy-done((bf16[1,512,1024]{2,1,0:T(8,128)(2,1)S(1)}, bf16[1,512,1024]{2,1,0:T(8,128)(2,1)}, u32[]{:S(2)}) %copy-start.1) | copy-done | bytes 1048600
  4.3 0.0 copy-start.9
  4.3 0.7 %copy-done.9 = s32[4]{0:T(128)S(1)} copy-done((s32[4]{0:T(128)S(1)}, s32[4]{0:T(128)}, u32[]{:S(2)}) %copy-start.9) | copy-done | bytes 40
  5.0 0.0 copy-start.10
  5.0 0.7 %copy-done.10 = s32[5]{0:T(128)S(1)} copy-done((s32[5]{0:T(128)S(1)}, s32[5]{0:T(128)}, u32[]{:S(2)}) %copy-start.10) | copy-done | bytes 44
  5.7 0.0 copy-start.11
  5.7 0.7 %copy-done.11 = s32[4]{0:T(128)S(1)} copy-done((s32[4]{0:T(128)S(1)}, s32[4]{0:T(128)}, u32[]{:S(2)}) %copy-start.11) | copy-done | bytes 40
  6.3 0.0 copy-start.12
  6.3 0.7 %copy-done.12 = s32[4]{0:T(128)S(1)} copy-done((s32[4]{0:T(128)S(1)}, s32[4]{0:T(128)}, u32[]{:S(2)}) %copy-start.12) | copy-done | bytes 40
  7.0 0.0 copy-start.6
  7.0 0.0 copy-start.7
  7.0 0.0 copy-start.8
  7.0 24.3 %project.1 = (bf16[4,256,256]{2,1,0:T(8,128)(2,1)S(1)}, f32[544,512]{1,0:T(8,128)S(1)}) custom-call(s32[4]{0:T(128)S(1)} %copy-done.9, s32[5]{0:T(128)S(1)} %copy-done.10, s32[4]{0:T(128)S(1)} %copy-done.11, s32[4]{0:T(128)S(1)} %copy-done.12, bf16[5,8,256,256]{3,2,1,0:T(8,128)(2,1)S(1)} %copy-done, bf16[1,512,1024]{2,1,0:T(8,128)(2,1)S(1)} %copy-done.1), custom_call_target="tpu_custom_call" | custom-call | tf_op jit(solution)/shard_map/project/pallas_call | solution.py:387
  31.3 0.0 copy-done.2
  31.3 0.0 copy-done.3
  31.3 0.0 copy-done.4
  31.4 0.0 copy-done.5
  31.4 0.0 copy-done.6
  31.4 0.0 copy-done.7
  31.4 0.0 copy-done.8
  31.4 6.4 %correlate.1 = (f32[1,512,512]{2,1,0:T(8,128)}, f32[1,512,512]{2,1,0:T(8,128)}, f32[1,512,512]{2,1,0:T(8,128)}) custom-call(bf16[4,256,256]{2,1,0:T(8,128)(2,1)S(1)} %get-tuple-element.5.template_ref, f32[544,512]{1,0:T(8,128)S(1)} %get-tuple-element.6.folded_ref, bf16[544,256]{1,0:T(8,128)(2,1)S(1)} %copy-done.7, bf16[2,256,512]{2,1,0:T(8,128)(2,1)S(1)} %copy-done.6, ...), custom_call_target="tpu_custom_call" | custom-call | tf_op jit(solution)/shard_map/correlate/pallas_call | solution.py:422
  (4 shorter events, 0.0 us)
Async XLA Ops:
  0.6 2.5 %copy-start = (bf16[5,8,256,256]{3,2,1,0:T(8,128)(2,1)S(1)}, bf16[5,8,256,256]{3,2,1,0:T(8,128)(2,1)}, u32[]{:S(2)}) copy-start(bf16[5,8,256,256]{3,2,1,0:T(8,128)(2,1)} %map_ref.1) | copy-start | bytes 15728644
  3.1 1.2 %copy-start.1 = (bf16[1,512,1024]{2,1,0:T(8,128)(2,1)S(1)}, bf16[1,512,1024]{2,1,0:T(8,128)(2,1)}, u32[]{:S(2)}) copy-start(bf16[1,512,1024]{2,1,0:T(8,128)(2,1)} %tile_ref.1) | copy-start | bytes 3145732
  4.3 0.7 %copy-start.9 = (s32[4]{0:T(128)S(1)}, s32[4]{0:T(128)}, u32[]{:S(2)}) copy-start(s32[4]{0:T(128)} %orient_ref.1) | copy-start | bytes 52
  5.0 0.7 %copy-start.10 = (s32[5]{0:T(128)S(1)}, s32[5]{0:T(128)}, u32[]{:S(2)}) copy-start(s32[5]{0:T(128)} %slot_ref.1) | copy-start | bytes 64
  5.7 0.7 %copy-start.11 = (s32[4]{0:T(128)S(1)}, s32[4]{0:T(128)}, u32[]{:S(2)}) copy-start(s32[4]{0:T(128)} %lo_ref.1) | copy-start | bytes 52
  6.3 0.7 %copy-start.12 = (s32[4]{0:T(128)S(1)}, s32[4]{0:T(128)}, u32[]{:S(2)}) copy-start(s32[4]{0:T(128)} %hi_ref.1) | copy-start | bytes 52
  7.0 24.4 %copy-start.2 = (f32[1,512,512]{2,1,0:T(8,128)S(1)}, f32[1,512,512]{2,1,0:T(8,128)}, u32[]{:S(2)}) copy-start(f32[1,512,512]{2,1,0:T(8,128)} %max_ref.1) | copy-start | bytes 3145732
  7.0 24.4 %copy-start.3 = (f32[1,512,512]{2,1,0:T(8,128)S(1)}, f32[1,512,512]{2,1,0:T(8,128)}, u32[]{:S(2)}) copy-start(f32[1,512,512]{2,1,0:T(8,128)} %sum_ref.1) | copy-start | bytes 3145732
  7.0 24.4 %copy-start.4 = (f32[1,512,512]{2,1,0:T(8,128)S(1)}, f32[1,512,512]{2,1,0:T(8,128)}, u32[]{:S(2)}) copy-start(f32[1,512,512]{2,1,0:T(8,128)} %sumsq_ref.1) | copy-start | bytes 3145732
  7.0 24.4 %copy-start.5 = (bf16[2,512,512]{2,1,0:T(8,128)(2,1)S(1)}, bf16[2,512,512]{2,1,0:T(8,128)(2,1)}, u32[]{:S(2)}) copy-start(bf16[2,512,512]{2,1,0:T(8,128)(2,1)} %constant.10.clone.inverse_ref) | copy-start | bytes 3145732
  7.0 24.4 %copy-start.6 = (bf16[2,256,512]{2,1,0:T(8,128)(2,1)S(1)}, bf16[2,256,512]{2,1,0:T(8,128)(2,1)}, u32[]{:S(2)}) copy-start(bf16[2,256,512]{2,1,0:T(8,128)(2,1)} %constant.9.clone.spread_ref) | copy-start | bytes 1572868
  7.0 24.4 %copy-start.7 = (bf16[544,256]{1,0:T(8,128)(2,1)S(1)}, bf16[544,256]{1,0:T(8,128)(2,1)}, u32[]{:S(2)}) copy-start(bf16[544,256]{1,0:T(8,128)(2,1)} %constant.8.clone.column_ref) | copy-start | bytes 835588
  7.0 24.4 %copy-start.8 = (bf16[2,256,256]{2,1,0:T(8,128)(2,1)S(1)}, bf16[2,256,256]{2,1,0:T(8,128)(2,1)}, u32[]{:S(2)}) copy-start(bf16[2,256,256]{2,1,0:T(8,128)(2,1)} %constant.11.clone.final_ref) | copy-start | bytes 786436

commit v2 on v1

--- a/solution.py
+++ b/solution.py
@@ -100,8 +100,8 @@
     hi_ref,
     map_ref,
     tile_ref,
-    template_ref,
-    folded_ref,
+    template,
+    folded,
     slabs,
     tile,
     rowsel,
@@ -113,12 +113,9 @@
     sib_recv,
     z_send,
     z_recv,
-    template,
     picked,
-    folded,
     in_sem,
     slab_sem,
-    out_sem,
     send_sem,
     recv_sem,
 ):
@@ -185,6 +182,7 @@
     acc[...] = jnp.zeros_like(acc)
 
     def one_slot(slot, carry):
+        pltpu.make_async_copy(map_ref.at[slot], slabs.at[slot], slab_sem.at[slot]).wait()
         slab = jnp.full((SLAB_Z, 128), slot_ref[slot])
         depth = (slab * SLAB_Z + within).astype(jnp.float32) - center
         inside = jnp.where((slab >= lo_ref[own]) & (slab < hi_ref[own]), 1.0, 0.0)
@@ -204,8 +202,6 @@
             at0, at1, at2 = (right_gap == row(ny + k, (BOX, 128)) for k in (0.0, 1.0, 2.0))
             right[j * BOX : (j + 1) * BOX, :128] = jnp.where(at0, w0, jnp.where(at1, w1, zero))
             right[j * BOX : (j + 1) * BOX, 128:] = jnp.where(at1, w0, jnp.where(at2, w1, zero))
-        pltpu.make_async_copy(map_ref.at[slot], slabs.at[slot], slab_sem.at[slot]).wait()
-        for j in range(SLAB_Z):
             sheared[:, j * BOX : (j + 1) * BOX] = dot(left[j], slabs[slot, j]).astype(jnp.bfloat16)
         acc[...] += dot(sheared[...], right[...])
         return carry
@@ -240,8 +236,6 @@
     hop = send(1, 1, z_send, z_recv, across)
     hop.start()
     folded[...] = dot(picked[...], colsel[...])
-    save = pltpu.make_async_copy(folded, folded_ref, out_sem.at[0])
-    save.start()
     hop.wait()
     template[own, mine, :] = (chip_sum + z_recv[...].astype(jnp.float32)).astype(jnp.bfloat16)
     block = template.at[own, mine]
@@ -258,31 +252,21 @@
         send(2, arrival, landed, landed, sibling).wait_recv()
     for hop in hops:
         hop.wait_send()
-    out = pltpu.make_async_copy(template, template_ref, out_sem.at[1])
-    out.start()
-    out.wait()
-    save.wait()
 
 
 def correlate_kernel(
-    template_ref,
-    folded_ref,
-    column_ref,
-    spread_ref,
-    inverse_ref,
-    final_ref,
+    template,
+    folded,
+    column,
+    spread,
+    inverse,
+    final,
     max_ref,
     sum_ref,
     sumsq_ref,
     out_max_ref,
     out_sum_ref,
     out_sumsq_ref,
-    template,
-    folded,
-    column,
-    spread,
-    inverse,
-    final,
     best,
     total,
     square,
@@ -291,37 +275,14 @@
     half,
     even_part,
     odd_part,
-    in_sem,
     out_sem,
 ):
-    copies = [
-        pltpu.make_async_copy(src, dst, in_sem.at[i])
-        for i, (src, dst) in enumerate(
-            (
-                (template_ref, template),
-                (column_ref, column),
-                (spread_ref, spread),
-                (folded_ref, folded),
-                (inverse_ref, inverse),
-                (final_ref, final),
-                (max_ref.at[0], best),
-                (sum_ref.at[0], total),
-                (sumsq_ref.at[0], square),
-            )
-        )
-    ]
-    for copy in copies:
-        copy.start()
-    copies[0].wait()
-    copies[1].wait()
     for o in range(ORI):
         value = dot(column[...], template[o]).astype(jnp.bfloat16)
         cs[o, :, 0:128] = value[:ROWS, :128]
         cs[o, :, 128:256] = value[ROWS:, :128]
         cs[o, :, 256:384] = value[:ROWS, 128:]
         cs[o, :, 384:512] = value[ROWS:, 128:]
-    copies[2].wait()
-    copies[3].wait()
     for o in range(ORI):
         for q in range(2):
             even = dot(cs[o, :, :256], spread[0, :, q * 256 : (q + 1) * 256])
@@ -338,7 +299,6 @@
                 top_im = im[:8] + re[BOX : BOX + 8]
                 prod[o, q, :8, h * 128 : (h + 1) * 128] = top_re.astype(jnp.bfloat16)
                 prod[o, q, :8, 256 + h * 128 : 256 + (h + 1) * 128] = top_im.astype(jnp.bfloat16)
-    copies[4].wait()
     for o in range(ORI):
         even = dot(prod[o, 0], inverse[0])
         odd = dot(prod[o, 1], inverse[1])
@@ -349,8 +309,6 @@
             half[o, parity, 128:, :256] = low[rows, 256:]
             half[o, parity, :128, 256:] = high[rows, :256]
             half[o, parity, 128:, 256:] = high[rows, 256:]
-    for copy in copies[5:]:
-        copy.wait()
     outs = []
     for block in range(2):
         lanes = slice(block * 256, (block + 1) * 256)
@@ -362,7 +320,7 @@
             rows = pl.ds(pl.multiple_of(i * 16, 16), 16)
             high_rows = pl.ds(pl.multiple_of(i * 16 + BOX, 16), 16)
             for sign, dest in ((1, rows), (-1, high_rows)):
-                peak, run, energy = best[dest, lanes], total[dest, lanes], square[dest, lanes]
+                peak, run, energy = max_ref[0, dest, lanes], sum_ref[0, dest, lanes], sumsq_ref[0, dest, lanes]
                 for o in range(ORI):
                     even, odd = even_part[o, rows, :], odd_part[o, rows, :]
                     score = even + odd if sign == 1 else even - odd
@@ -384,15 +342,16 @@
     smem = pl.BlockSpec(memory_space=pltpu.SMEM)
     hbm = pl.BlockSpec(memory_space=pl.ANY)
     vmem = pltpu.VMEM
+    in_hbm = lambda a: pltpu.with_memory_space_constraint(a, pltpu.HBM)
     template, folded = pl.pallas_call(
         project_kernel,
         name="project",
         out_shape=(
-            jax.ShapeDtypeStruct((ORI, BOX, BOX), jnp.bfloat16),
-            jax.ShapeDtypeStruct((2 * ROWS, TILE), jnp.float32),
+            vmem((ORI, BOX, BOX), jnp.bfloat16),
+            vmem((2 * ROWS, TILE), jnp.float32),
         ),
         in_specs=[smem] * 4 + [hbm] * 2,
-        out_specs=(hbm, hbm),
+        out_specs=(pl.BlockSpec(memory_space=vmem),) * 2,
         scratch_shapes=[
             vmem((SLOTS, SLAB_Z, BOX, BOX), jnp.bfloat16),
             vmem((TILE, 2 * TILE), jnp.bfloat16),
@@ -405,33 +364,24 @@
             vmem((HALF, BOX), jnp.float32),
             vmem((HALF, BOX), jnp.bfloat16),
             vmem((HALF, BOX), jnp.bfloat16),
-            vmem((ORI, BOX, BOX), jnp.bfloat16),
             vmem((2 * ROWS, 2 * TILE), jnp.bfloat16),
-            vmem((2 * ROWS, TILE), jnp.float32),
             pltpu.SemaphoreType.DMA((1,)),
             pltpu.SemaphoreType.DMA((SLOTS,)),
-            pltpu.SemaphoreType.DMA((2,)),
             pltpu.SemaphoreType.DMA((9,)),
             pltpu.SemaphoreType.DMA((9,)),
         ],
         compiler_params=pltpu.CompilerParams(
-            collective_id=0, has_side_effects=True, vmem_limit_bytes=40 << 20
+            collective_id=0, has_side_effects=True, vmem_limit_bytes=50 << 20
         ),
-    )(orient_index, slot_slab, slab_lo, slab_hi, map_slabs, tile_spectrum)
+    )(*(in_hbm(a) for a in (orient_index, slot_slab, slab_lo, slab_hi)), in_hbm(map_slabs), in_hbm(tile_spectrum))
     plane = jax.ShapeDtypeStruct((1, TILE, TILE), jnp.float32)
     return pl.pallas_call(
         correlate_kernel,
         name="correlate",
         out_shape=(plane, plane, plane),
-        in_specs=[hbm] * 9,
+        in_specs=[pl.BlockSpec(memory_space=vmem)] * 9,
         out_specs=(hbm, hbm, hbm),
         scratch_shapes=[
-            vmem((ORI, BOX, BOX), jnp.bfloat16),
-            vmem((2 * ROWS, TILE), jnp.float32),
-            vmem((2 * ROWS, BOX), jnp.bfloat16),
-            vmem((2, BOX, TILE), jnp.bfloat16),
-            vmem((2, TILE, TILE), jnp.bfloat16),
-            vmem((2, BOX, BOX), jnp.bfloat16),
             vmem((TILE, TILE), jnp.float32),
             vmem((TILE, TILE), jnp.float32),
             vmem((TILE, TILE), jnp.float32),
@@ -440,7 +390,6 @@
             vmem((ORI, 2, BOX, TILE), jnp.bfloat16),
             vmem((ORI, BOX, BOX), jnp.float32),
             vmem((ORI, BOX, BOX), jnp.float32),
-            pltpu.SemaphoreType.DMA((9,)),
             pltpu.SemaphoreType.DMA((6,)),
         ],
         compiler_params=pltpu.CompilerParams(vmem_limit_bytes=40 << 20),

time: 38 us -> 29.1 us (0.77)
  local copies, waits for them, and re-layouts: 6.36 us -> 0.04 us
  Pallas kernels: 30.7 us -> 28.2 us
    unnamed x26 -> x14, local copies, waits for them, and re-layouts: 6.36 us -> 0.04 us
    pallas_call x1, Pallas kernels: 24.3 us -> 23 us  [body(): pl.pallas_call(project_kernel, name='project', out_shape=(vmem((ORI, BOX,...]
    pallas_call x1, Pallas kernels: 6.37 us -> 5.17 us  [body(): pl.pallas_call(correlate_kernel, name='correlate', out_shape=(plane, plan...]
where the time goes in v2:
time: 29.1 us; the launch traced here: 29 us
  Pallas kernels  28.2 us (97%)
  between operations  0.75 us (3%)
    pallas_call x1, Pallas kernels, body(): pl.pallas_call(project_kernel, name='project', out_shape=(vmem((ORI, BOX,...  23 us
    pallas_call x1, Pallas kernels, body(): pl.pallas_call(correlate_kernel, name='correlate', out_shape=(plane, plan...  5.17 us

profile of v2, /device:TPU:1, one launch (start us, length us, event | category | flops | bytes accessed | tf_op | source)
XLA Modules:
  0.0 29.0 jit_solution(14604903675196485534)
XLA Ops:
  0.6 0.0 copy-start.6
  0.6 0.0 copy-start.3
  0.7 0.0 copy-start.4
  0.7 0.0 copy-start.5
  0.7 0.0 copy-start.2
  0.7 0.0 copy-start.1
  0.7 0.0 copy-start
  0.7 23.0 %project.1 = (bf16[4,256,256]{2,1,0:T(8,128)(2,1)S(1)}, f32[544,512]{1,0:T(8,128)S(1)}) custom-call(s32[4]{0:T(128)} %orient_ref.1, s32[5]{0:T(128)} %slot_ref.1, s32[4]{0:T(128)} %lo_ref.1, s32[4]{0:T(128)} %hi_ref.1, bf16[5,8,256,256]{3,2,1,0:T(8,128)(2,1)} %map_ref.1, bf16[1,512,1024]{2,1,0:T(8,128)(2,1)} %tile_ref.1), custom_call_target="tpu_custom_call" | custom-call | tf_op jit(solution)/shard_map/project/pallas_call | solution.py:346
  23.8 0.0 copy-done.6
  23.8 0.0 copy-done.3
  23.8 0.0 copy-done.4
  23.8 0.0 copy-done.5
  23.8 0.0 copy-done.2
  23.8 0.0 copy-done.1
  23.8 0.0 copy-done
  23.8 5.2 %correlate.1 = (f32[1,512,512]{2,1,0:T(8,128)}, f32[1,512,512]{2,1,0:T(8,128)}, f32[1,512,512]{2,1,0:T(8,128)}) custom-call(bf16[4,256,256]{2,1,0:T(8,128)(2,1)S(1)} %get-tuple-element.5.template, f32[544,512]{1,0:T(8,128)S(1)} %get-tuple-element.6.folded, bf16[544,256]{1,0:T(8,128)(2,1)S(1)} %copy-done.5, bf16[2,256,512]{2,1,0:T(8,128)(2,1)S(1)} %copy-done.4, ...), custom_call_target="tpu_custom_call" | custom-call | tf_op jit(solution)/shard_map/correlate/pallas_call | solution.py:378
Async XLA Ops:
  0.6 23.1 %copy-start.6 = (bf16[2,256,256]{2,1,0:T(8,128)(2,1)S(1)}, bf16[2,256,256]{2,1,0:T(8,128)(2,1)}, u32[]{:S(2)}) copy-start(bf16[2,256,256]{2,1,0:T(8,128)(2,1)} %constant.11.clone.final) | copy-start | bytes 786436
  0.6 23.1 %copy-start.3 = (bf16[2,512,512]{2,1,0:T(8,128)(2,1)S(1)}, bf16[2,512,512]{2,1,0:T(8,128)(2,1)}, u32[]{:S(2)}) copy-start(bf16[2,512,512]{2,1,0:T(8,128)(2,1)} %constant.10.clone.inverse) | copy-start | bytes 3145732
  0.7 23.1 %copy-start.4 = (bf16[2,256,512]{2,1,0:T(8,128)(2,1)S(1)}, bf16[2,256,512]{2,1,0:T(8,128)(2,1)}, u32[]{:S(2)}) copy-start(bf16[2,256,512]{2,1,0:T(8,128)(2,1)} %constant.9.clone.spread) | copy-start | bytes 1572868
  0.7 23.1 %copy-start.5 = (bf16[544,256]{1,0:T(8,128)(2,1)S(1)}, bf16[544,256]{1,0:T(8,128)(2,1)}, u32[]{:S(2)}) copy-start(bf16[544,256]{1,0:T(8,128)(2,1)} %constant.8.clone.column) | copy-start | bytes 835588
  0.7 23.1 %copy-start.2 = (f32[1,512,512]{2,1,0:T(8,128)S(1)}, f32[1,512,512]{2,1,0:T(8,128)}, u32[]{:S(2)}) copy-start(f32[1,512,512]{2,1,0:T(8,128)} %sumsq_ref.1) | copy-start | bytes 3145732
  0.7 23.1 %copy-start.1 = (f32[1,512,512]{2,1,0:T(8,128)S(1)}, f32[1,512,512]{2,1,0:T(8,128)}, u32[]{:S(2)}) copy-start(f32[1,512,512]{2,1,0:T(8,128)} %sum_ref.1) | copy-start | bytes 3145732
  0.7 23.1 %copy-start = (f32[1,512,512]{2,1,0:T(8,128)S(1)}, f32[1,512,512]{2,1,0:T(8,128)}, u32[]{:S(2)}) copy-start(f32[1,512,512]{2,1,0:T(8,128)} %max_ref.1) | copy-start | bytes 3145732
